TPU v7x, 32 devices: a whole 2x2x4 slice. The times are simulated.
32 devices in a mesh: ctx: 16 (over z, x, core), fsdp: 2 (over y).
Axes of the slice: x: 2, y: 2, z: 4, core: 2. Of those that a mesh axis runs over, the one named last changes fastest.
Arguments:
- tokens: bfloat16 [2, 4096, 768], P('fsdp', 'ctx'), may hold values from -6 to 6
- query_weight: bfloat16 [768, 768], P('fsdp'), may hold values from -0.21875 to 0.21875
- query_bias: bfloat16 [768], P('fsdp'), may hold values from -1.5 to 1.5
- key_weight: bfloat16 [768, 768], P('fsdp'), may hold values from -0.21875 to 0.21875
- value_weight: bfloat16 [768, 768], P('fsdp'), may hold values from -0.21875 to 0.21875
- value_bias: bfloat16 [768], P('fsdp'), may hold values from -1.5 to 1.5
- out_weight: bfloat16 [768, 768], P('fsdp'), may hold values from -1.25 to 1.25
- out_bias: bfloat16 [768], P('fsdp'), may hold values from -1.5 to 1.5
- first_gain: bfloat16 [768], P('fsdp'), may hold values from 0.5 to 1.5
- first_shift: bfloat16 [768], P('fsdp'), may hold values from -1.5 to 1.5
- inner_weight: bfloat16 [768, 3072], P('fsdp'), may hold values from -0.21875 to 0.21875
- inner_bias: bfloat16 [3072], P('fsdp'), may hold values from -1.5 to 1.5
- outer_weight: bfloat16 [3072, 768], P('fsdp'), may hold values from -0.109375 to 0.109375
- outer_bias: bfloat16 [768], P('fsdp'), may hold values from -1.5 to 1.5
- second_gain: bfloat16 [768], P('fsdp'), may hold values from 0.5 to 1.5
- second_shift: bfloat16 [768], P('fsdp'), may hold values from -1.5 to 1.5
- doc_lengths: int32 [2, 48], P('fsdp'), may hold values from 1 to 2304, 4096 in all within a row
- grad_output: bfloat16 [2, 4096, 768], P('fsdp', 'ctx'), may hold values from -6 to 6
Outputs:
- output: bfloat16 [2, 4096, 768], P('fsdp', 'ctx')
- grad_tokens: float32 [2, 4096, 768], P('fsdp', 'ctx')
- grad_query_weight: float32 [768, 768], P('fsdp')
- grad_query_bias: float32 [768], P('fsdp')
- grad_key_weight: float32 [768, 768], P('fsdp')
- grad_value_weight: float32 [768, 768], P('fsdp')
- grad_value_bias: float32 [768], P('fsdp')
- grad_out_weight: float32 [768, 768], P('fsdp')
- grad_out_bias: float32 [768], P('fsdp')
- grad_first_gain: float32 [768], P('fsdp')
- grad_first_shift: float32 [768], P('fsdp')
- grad_inner_weight: float32 [768, 3072], P('fsdp')
- grad_inner_bias: float32 [3072], P('fsdp')
- grad_outer_weight: float32 [3072, 768], P('fsdp')
- grad_outer_bias: float32 [768], P('fsdp')
- grad_second_gain: float32 [768], P('fsdp')
- grad_second_shift: float32 [768], P('fsdp')
Inputs may be any that keep to these rules, and one draw needn't show every extreme that they name: `doc_lengths`: each row holds the 48 document lengths of one sequence in order; they sum to 4096 and the longest is exactly 2304.
All inputs are finite; a program needn't handle non-finite values.
Results may differ from a plain program's by a relative error of at most 0.018.
Values may be sent and summed in bfloat16 or wider, within the bound.
No kernel may reach another device: no remote copies, remote signals or barrier semaphores. Data moves between devices by JAX's collectives and lax.ppermute only.
A program may use at most 384 MiB of HBM per device.

v0:
```python
import math
import jax
import jax.numpy as jnp
from jax import lax
from jax.sharding import PartitionSpec as P

H = 12
HD = 64
eps = 1e-12


def layer_norm(r, gain, shift):
    mean = jnp.mean(r, axis=-1, keepdims=True)
    centered = r - mean
    var = jnp.mean(centered * centered, axis=-1, keepdims=True)
    return centered * lax.rsqrt(var + eps) * gain + shift


def gelu_exact(v):
    return jax.nn.gelu(v, approximate=False)


def inner_rows(left, right):
    return lax.dot_general(
        left, right, (((1,), (1,)), ((), ())), preferred_element_type=jnp.float32
    )


def inner_cols(left, right):
    return lax.dot_general(
        left, right, (((0,), (0,)), ((), ())), preferred_element_type=jnp.float32
    )


def segment_of(places, lengths):
    ends = jnp.cumsum(lengths)
    return jnp.sum((places[:, None] >= ends[None, :]).astype(jnp.int32), axis=1)


def masked_scores(query_part, key_part, allowed, scale):
    raw = inner_rows(query_part, key_part) * scale
    return jnp.where(allowed, raw, jnp.float32(-1e30))


def on_device(
    tokens,
    query_weight,
    query_bias,
    key_weight,
    value_weight,
    value_bias,
    out_weight,
    out_bias,
    first_gain,
    first_shift,
    inner_weight,
    inner_bias,
    outer_weight,
    outer_bias,
    second_gain,
    second_shift,
    doc_lengths,
    grad_output,
):
    rows = tokens.shape[1]
    width = tokens.shape[2]
    scale = 1.0 / math.sqrt(HD)
    length_total = rows * lax.axis_size("ctx")
    gathered = (
        lax.all_gather(query_weight, "fsdp", axis=0, tiled=True),
        lax.all_gather(query_bias, "fsdp", axis=0, tiled=True),
        lax.all_gather(key_weight, "fsdp", axis=0, tiled=True),
        lax.all_gather(value_weight, "fsdp", axis=0, tiled=True),
        lax.all_gather(value_bias, "fsdp", axis=0, tiled=True),
        lax.all_gather(out_weight, "fsdp", axis=0, tiled=True),
        lax.all_gather(out_bias, "fsdp", axis=0, tiled=True),
        lax.all_gather(first_gain, "fsdp", axis=0, tiled=True),
        lax.all_gather(first_shift, "fsdp", axis=0, tiled=True),
        lax.all_gather(inner_weight, "fsdp", axis=0, tiled=True),
        lax.all_gather(inner_bias, "fsdp", axis=0, tiled=True),
        lax.all_gather(outer_weight, "fsdp", axis=0, tiled=True),
        lax.all_gather(outer_bias, "fsdp", axis=0, tiled=True),
        lax.all_gather(second_gain, "fsdp", axis=0, tiled=True),
        lax.all_gather(second_shift, "fsdp", axis=0, tiled=True),
    )
    (
        query_full,
        qbias_full,
        key_full,
        value_full,
        vbias_full,
        out_full,
        obias_full,
        gain_one,
        shift_one,
        inner_full,
        ibias_full,
        outer_full,
        outbias_full,
        gain_two,
        shift_two,
    ) = gathered
    local_in = tokens[0]
    local_float = local_in.astype(jnp.float32)
    query_low = (
        jnp.dot(local_in, query_full, preferred_element_type=jnp.float32)
        + qbias_full.astype(jnp.float32)
    ).astype(jnp.bfloat16)
    key_low = jnp.dot(local_in, key_full, preferred_element_type=jnp.float32).astype(jnp.bfloat16)
    value_low = (
        jnp.dot(local_in, value_full, preferred_element_type=jnp.float32)
        + vbias_full.astype(jnp.float32)
    ).astype(jnp.bfloat16)
    first_row = lax.axis_index("ctx") * rows
    places_own = first_row + jnp.arange(rows, dtype=jnp.int32)
    segs_own = segment_of(places_own, doc_lengths[0])
    keys_all, values_all = (
        lax.all_gather(key_low, "ctx", axis=0, tiled=True),
        lax.all_gather(value_low, "ctx", axis=0, tiled=True),
    )
    places_all = jnp.arange(length_total, dtype=jnp.int32)
    segs_all = segment_of(places_all, doc_lengths[0])
    allowed = segs_own[:, None] == segs_all[None, :]
    head_outs = []
    log_list = []
    for head in range(H):
        cols = slice(head * HD, (head + 1) * HD)
        scores = masked_scores(query_low[:, cols], keys_all[:, cols], allowed, scale)
        top = jnp.max(scores, axis=1, keepdims=True)
        expd = jnp.exp(scores - top)
        total = jnp.sum(expd, axis=1, keepdims=True)
        probs_low = (expd / total).astype(jnp.bfloat16)
        head_outs.append(
            jnp.dot(probs_low, values_all[:, cols], preferred_element_type=jnp.float32)
        )
        log_list.append(top[:, 0] + jnp.log(total[:, 0]))
    attn_low = jnp.concatenate(head_outs, axis=1).astype(jnp.bfloat16)
    log_sums = jnp.stack(log_list, axis=0)
    branch = jnp.dot(attn_low, out_full, preferred_element_type=jnp.float32) + obias_full.astype(
        jnp.float32
    )
    hidden, first_back = jax.vjp(
        layer_norm,
        local_float + branch,
        gain_one.astype(jnp.float32),
        shift_one.astype(jnp.float32),
    )
    hidden_low = hidden.astype(jnp.bfloat16)
    inner = jnp.dot(hidden_low, inner_full, preferred_element_type=jnp.float32) + ibias_full.astype(
        jnp.float32
    )
    active, gelu_back = jax.vjp(gelu_exact, inner)
    active_low = active.astype(jnp.bfloat16)
    outer = jnp.dot(
        active_low, outer_full, preferred_element_type=jnp.float32
    ) + outbias_full.astype(jnp.float32)
    result, second_back = jax.vjp(
        layer_norm, hidden + outer, gain_two.astype(jnp.float32), shift_two.astype(jnp.float32)
    )
    output = result.astype(jnp.bfloat16)[None]
    grad_y = grad_output[0].astype(jnp.float32)
    d_second, grad_gain_two, grad_shift_two = second_back(grad_y)
    d_outer_low = d_second.astype(jnp.bfloat16)
    grad_outbias = jnp.sum(d_outer_low.astype(jnp.float32), axis=0)
    grad_outer = inner_cols(active_low, d_outer_low)
    d_active = inner_rows(d_outer_low, outer_full)
    (d_inner,) = gelu_back(d_active)
    d_inner_low = d_inner.astype(jnp.bfloat16)
    grad_ibias = jnp.sum(d_inner_low.astype(jnp.float32), axis=0)
    grad_inner = inner_cols(hidden_low, d_inner_low)
    d_hidden = d_second + inner_rows(d_inner_low, inner_full)
    d_first, grad_gain_one, grad_shift_one = first_back(d_hidden)
    d_branch_low = d_first.astype(jnp.bfloat16)
    grad_obias = jnp.sum(d_branch_low.astype(jnp.float32), axis=0)
    grad_out = inner_cols(attn_low, d_branch_low)
    d_attn_low = inner_rows(d_branch_low, out_full).astype(jnp.bfloat16)
    dq_list = []
    dk_list = []
    dv_list = []
    for head in range(H):
        cols = slice(head * HD, (head + 1) * HD)
        scores = masked_scores(query_low[:, cols], keys_all[:, cols], allowed, scale)
        probs = jnp.exp(scores - log_sums[head][:, None])
        d_probs = inner_rows(d_attn_low[:, cols], values_all[:, cols])
        delta = jnp.sum(probs * d_probs, axis=1)
        d_scores = (probs * (d_probs - delta[:, None])).astype(jnp.bfloat16)
        dq_list.append(
            jnp.dot(d_scores, keys_all[:, cols], preferred_element_type=jnp.float32) * scale
        )
        dk_list.append(inner_cols(d_scores, query_low[:, cols]) * scale)
        dv_list.append(inner_cols(probs.astype(jnp.bfloat16), d_attn_low[:, cols]))
    key_terms = jnp.concatenate(dk_list + dv_list, axis=1)
    shares = lax.psum_scatter(
        key_terms.astype(jnp.bfloat16), "ctx", scatter_dimension=0, tiled=True
    ).astype(jnp.float32)
    d_key_low = shares[:, :width].astype(jnp.bfloat16)
    d_value_low = shares[:, width:].astype(jnp.bfloat16)
    d_query_low = jnp.concatenate(dq_list, axis=1).astype(jnp.bfloat16)
    grad_qbias = jnp.sum(d_query_low.astype(jnp.float32), axis=0)
    grad_vbias = jnp.sum(d_value_low.astype(jnp.float32), axis=0)
    grad_query = inner_cols(local_in, d_query_low)
    grad_key = inner_cols(local_in, d_key_low)
    grad_value = inner_cols(local_in, d_value_low)
    grad_input = (
        d_first
        + inner_rows(d_query_low, query_full)
        + inner_rows(d_key_low, key_full)
        + inner_rows(d_value_low, value_full)
    )
    shards = (
        lax.psum_scatter(
            grad_query.astype(jnp.bfloat16), "fsdp", scatter_dimension=0, tiled=True
        ).astype(jnp.float32),
        lax.psum_scatter(
            grad_qbias.astype(jnp.bfloat16), "fsdp", scatter_dimension=0, tiled=True
        ).astype(jnp.float32),
        lax.psum_scatter(
            grad_key.astype(jnp.bfloat16), "fsdp", scatter_dimension=0, tiled=True
        ).astype(jnp.float32),
        lax.psum_scatter(
            grad_value.astype(jnp.bfloat16), "fsdp", scatter_dimension=0, tiled=True
        ).astype(jnp.float32),
        lax.psum_scatter(
            grad_vbias.astype(jnp.bfloat16), "fsdp", scatter_dimension=0, tiled=True
        ).astype(jnp.float32),
        lax.psum_scatter(
            grad_out.astype(jnp.bfloat16), "fsdp", scatter_dimension=0, tiled=True
        ).astype(jnp.float32),
        lax.psum_scatter(
            grad_obias.astype(jnp.bfloat16), "fsdp", scatter_dimension=0, tiled=True
        ).astype(jnp.float32),
        lax.psum_scatter(
            grad_gain_one.astype(jnp.bfloat16), "fsdp", scatter_dimension=0, tiled=True
        ).astype(jnp.float32),
        lax.psum_scatter(
            grad_shift_one.astype(jnp.bfloat16), "fsdp", scatter_dimension=0, tiled=True
        ).astype(jnp.float32),
        lax.psum_scatter(
            grad_inner.astype(jnp.bfloat16), "fsdp", scatter_dimension=0, tiled=True
        ).astype(jnp.float32),
        lax.psum_scatter(
            grad_ibias.astype(jnp.bfloat16), "fsdp", scatter_dimension=0, tiled=True
        ).astype(jnp.float32),
        lax.psum_scatter(
            grad_outer.astype(jnp.bfloat16), "fsdp", scatter_dimension=0, tiled=True
        ).astype(jnp.float32),
        lax.psum_scatter(
            grad_outbias.astype(jnp.bfloat16), "fsdp", scatter_dimension=0, tiled=True
        ).astype(jnp.float32),
        lax.psum_scatter(
            grad_gain_two.astype(jnp.bfloat16), "fsdp", scatter_dimension=0, tiled=True
        ).astype(jnp.float32),
        lax.psum_scatter(
            grad_shift_two.astype(jnp.bfloat16), "fsdp", scatter_dimension=0, tiled=True
        ).astype(jnp.float32),
    )
    totals = lax.psum(tuple(shards), "ctx")
    return (output, grad_input[None]) + tuple(totals)


def solution(mesh):
    placed = (
        P("fsdp", "ctx", None),
        P("fsdp", None),
        P("fsdp"),
        P("fsdp", None),
        P("fsdp", None),
        P("fsdp"),
        P("fsdp", None),
        P("fsdp"),
        P("fsdp"),
        P("fsdp"),
        P("fsdp", None),
        P("fsdp"),
        P("fsdp", None),
        P("fsdp"),
        P("fsdp"),
        P("fsdp"),
        P("fsdp", None),
        P("fsdp", "ctx", None),
    )
    return jax.shard_map(
        on_device,
        mesh=mesh,
        in_specs=placed,
        out_specs=(
            P("fsdp", "ctx", None),
            P("fsdp", "ctx", None),
            P("fsdp", None),
            P("fsdp"),
            P("fsdp", None),
            P("fsdp", None),
            P("fsdp"),
            P("fsdp", None),
            P("fsdp"),
            P("fsdp"),
            P("fsdp"),
            P("fsdp", None),
            P("fsdp"),
            P("fsdp", None),
            P("fsdp"),
            P("fsdp"),
            P("fsdp"),
        ),
        check_vma=False,
    )
```

profile of v0, /device:TPU:1, one launch (start us, length us, event | category | flops | bytes accessed | tf_op | source)
XLA Modules:
  0.0 1196.2 jit_solution(10272641338332044763)
XLA Ops:
  9.5 25.0 %all-gather.20.cloned.1.call-done = bf16[768,768]{1,0:T(8,128)(2,1)} async-done(((bf16[384,768]{1,0:T(8,128)(2,1)}), bf16[768,768]{1,0:T(8,128)(2,1)}) %all-gather.20.cloned.1.call-update) | async-done | bytes 1179664 | tf_op jit(solution)/shard_map/all_gather | solution.py:72
  41.2 17.6 %all-gather.24.cloned.1.call-done = bf16[768,768]{1,0:T(8,128)(2,1)} async-done(((bf16[384,768]{1,0:T(8,128)(2,1)}), bf16[768,768]{1,0:T(8,128)(2,1)}) %all-gather.24.cloned.1.call-update) | async-done | bytes 1179664 | tf_op jit(solution)/shard_map/all_gather | solution.py:73
  93.4 54.9 %all-gather.22.cloned.1.call-done = bf16[4096,768]{1,0:T(8,128)(2,1)} async-done(((bf16[256,768]{1,0:T(8,128)(2,1)}), bf16[4096,768]{1,0:T(8,128)(2,1)}) %all-gather.22.cloned.1.call-update) | async-done | bytes 6291472 | tf_op jit(solution)/shard_map/all_gather | solution.py:118
  194.7 16.8 %all-gather.26.cloned.1.call-done = bf16[4096,768]{1,0:T(8,128)(2,1)} async-done(((bf16[256,768]{1,0:T(8,128)(2,1)}), bf16[4096,768]{1,0:T(8,128)(2,1)}) %all-gather.26.cloned.1.call-update) | async-done | bytes 6291472 | tf_op jit(solution)/shard_map/all_gather | solution.py:119
  243.4 54.8 %all-gather.30.cloned.1.call-done = bf16[768,3072]{1,0:T(8,128)(2,1)} async-done(((bf16[384,3072]{1,0:T(8,128)(2,1)}), bf16[768,3072]{1,0:T(8,128)(2,1)}) %all-gather.30.cloned.1.call-update) | async-done | bytes 4718608 | tf_op jit(solution)/shard_map/all_gather | solution.py:79
  298.2 11.5 multiply_convert_fusion.12
  309.7 52.7 %all-gather.32.cloned.1.call-done = bf16[3072,768]{1,0:T(8,128)(2,1)} async-done(((bf16[1536,768]{1,0:T(8,128)(2,1)}), bf16[3072,768]{1,0:T(8,128)(2,1)}) %all-gather.32.cloned.1.call-update) | async-done | bytes 4718608 | tf_op jit(solution)/shard_map/all_gather | solution.py:81
  423.8 5.6 multiply_reduce_fusion.4
  429.4 6.4 multiply_convert_fusion.4
  441.1 6.0 multiply_convert_fusion.3
  447.1 5.6 multiply_reduce_fusion.2
  452.6 5.9 multiply_convert_fusion.2
  463.9 6.0 multiply_convert_fusion.1
  469.9 5.6 multiply_reduce_fusion
  475.5 5.9 multiply_convert_fusion
  560.3 93.9 %reduce-scatter.14.cloned.1.call-done = bf16[256,1536]{0,1:T(8,128)(2,1)} async-done(((bf16[4096,1536]{0,1:T(8,128)(2,1)}), bf16[256,1536]{0,1:T(8,128)(2,1)}) %reduce-scatter.14.cloned.1.call-update) | async-done | bytes 786448 | tf_op jit(solution)/shard_map/reduce_scatter | solution.py:193
  668.9 9.7 reduce-scatter.22.cloned.1.call-done
  679.9 22.8 %reduce-scatter.16.cloned.1.call-done = bf16[384,768]{1,0:T(8,128)(2,1)} async-done(((bf16[768,768]{1,0:T(8,128)(2,1)}), bf16[384,768]{1,0:T(8,128)(2,1)}) %reduce-scatter.16.cloned.1.call-update) | async-done | bytes 589840 | tf_op jit(solution)/shard_map/reduce_scatter | solution.py:226
  702.7 62.7 %reduce-scatter.18.cloned.1.call-done = bf16[384,3072]{1,0:T(8,128)(2,1)} async-done(((bf16[768,3072]{1,0:T(8,128)(2,1)}), bf16[384,3072]{1,0:T(8,128)(2,1)}) %reduce-scatter.18.cloned.1.call-update) | async-done | bytes 2359312 | tf_op jit(solution)/shard_map/reduce_scatter | solution.py:238
  765.4 63.0 %reduce-scatter.20.cloned.1.call-done = bf16[1536,768]{1,0:T(8,128)(2,1)} async-done(((bf16[3072,768]{1,0:T(8,128)(2,1)}), bf16[1536,768]{1,0:T(8,128)(2,1)}) %reduce-scatter.20.cloned.1.call-update) | async-done | bytes 2359312 | tf_op jit(solution)/shard_map/reduce_scatter | solution.py:244
  828.6 6.1 all-reduce.10
  841.4 11.6 reduce-scatter.24.cloned.1.call-done
  854.4 23.1 %reduce-scatter.26.cloned.1.call-done = bf16[384,768]{1,0:T(8,128)(2,1)} async-done(((bf16[768,768]{1,0:T(8,128)(2,1)}), bf16[384,768]{1,0:T(8,128)(2,1)}) %reduce-scatter.26.cloned.1.call-update) | async-done | bytes 589840
  878.8 303.9 %all-reduce.12 = (f32[384,768]{0,1:T(8,128)}, f32[384]{0:T(512)}, f32[384,768]{0,1:T(8,128)}, f32[384,768]{0,1:T(8,128)S(1)}, f32[384]{0:T(512)}, /*index=5*/f32...) all-reduce(bf16[384,768]{0,1:T(8,128)(2,1)S(1)} %copy.52, ...), channel_id=1, replica_groups=mesh['ctx'=16,'fsdp'=2] {'ctx'}, use_global_device_ids=true, to_apply=%region_49.50 | all-reduce | flops 3543552 | bytes 21270528 | tf_op jit(solution)/shard_map/psum | solution.py:257
  (427 shorter events, 302.6 us)
Async XLA Ops:
  7.2 27.3 %all-gather.20.cloned.1.call-start = ((), (), s32[]{:S(2)}) async-start(), calls=%async_computation.8 | async-start | bytes 1769472 | tf_op jit(solution)/shard_map/all_gather | solution.py:72
  7.9 50.9 %all-gather.24.cloned.1.call-start = ((), (), s32[]{:S(2)}) async-start(), calls=%async_computation.10 | async-start | bytes 1769472 | tf_op jit(solution)/shard_map/all_gather | solution.py:73
  8.7 82.9 %all-gather.18.cloned.1.call-start = ((), (), s32[]{:S(2)}) async-start(), calls=%async_computation.7 | async-start | bytes 1769472 | tf_op jit(solution)/shard_map/all_gather | solution.py:70
  9.4 138.9 %all-gather.22.cloned.1.call-start = ((), (), s32[]{:S(2)}) async-start(), calls=%async_computation.9 | async-start | bytes 6684672 | tf_op jit(solution)/shard_map/all_gather | solution.py:118
  37.1 40.7 %copy-start.85 = (bf16[384]{0:T(512)(128)(2,1)S(1)}, bf16[384]{0:T(512)(128)(2,1)}, u32[]{:S(2)}) copy-start(bf16[384]{0:T(512)(128)(2,1)} %param.27) | copy-start | bytes 2308
  37.1 44.2 %copy-start.86 = (bf16[384]{0:T(512)(128)(2,1)S(1)}, bf16[384]{0:T(512)(128)(2,1)}, u32[]{:S(2)}) copy-start(bf16[384]{0:T(512)(128)(2,1)} %param.26) | copy-start | bytes 2308
  37.2 47.4 %copy-start.87 = (bf16[384]{0:T(512)(128)(2,1)S(1)}, bf16[384]{0:T(512)(128)(2,1)}, u32[]{:S(2)}) copy-start(bf16[384]{0:T(512)(128)(2,1)} %param.32) | copy-start | bytes 2308
  37.2 50.7 %copy-start.88 = (bf16[384]{0:T(512)(128)(2,1)S(1)}, bf16[384]{0:T(512)(128)(2,1)}, u32[]{:S(2)}) copy-start(bf16[384]{0:T(512)(128)(2,1)} %param.33) | copy-start | bytes 2308
  37.2 54.4 %copy-start.57 = (bf16[1,256,768]{2,1,0:T(8,128)(2,1)S(1)}, bf16[1,256,768]{2,1,0:T(8,128)(2,1)}, u32[]{:S(2)}) copy-start(bf16[1,256,768]{2,1,0:T(8,128)(2,1)} %param.18) | copy-start | bytes 1179652
  37.2 174.3 %all-gather.26.cloned.1.call-start = ((), (), s32[]{:S(2)}) async-start(), calls=%async_computation.11 | async-start | bytes 6684672 | tf_op jit(solution)/shard_map/all_gather | solution.py:119
  61.5 179.4 %all-gather.28.cloned.1.call-start = ((), (), s32[]{:S(2)}) async-start(), calls=%async_computation.12 | async-start | bytes 1769472 | tf_op jit(solution)/shard_map/all_gather | solution.py:75
  62.0 236.2 %all-gather.30.cloned.1.call-start = ((), (), s32[]{:S(2)}) async-start(), calls=%async_computation.13 | async-start | bytes 7077888 | tf_op jit(solution)/shard_map/all_gather | solution.py:79
  62.8 299.6 %all-gather.32.cloned.1.call-start = ((), (), s32[]{:S(2)}) async-start(), calls=%async_computation.14 | async-start | bytes 7077888 | tf_op jit(solution)/shard_map/all_gather | solution.py:81
  63.5 590.6 %reduce-scatter.14.cloned.1.call-start = ((), (), s32[]{:S(2)}) async-start(), calls=%async_computation.15 | async-start | bytes 13369344 | tf_op jit(solution)/shard_map/reduce_scatter | solution.py:193
  93.4 57.8 %copy-start.78 = (bf16[256,768]{1,0:T(8,128)(2,1)}, bf16[256,768]{1,0:T(8,128)(2,1)S(1)}, u32[]{:S(2)}) copy-start(bf16[256,768]{1,0:T(8,128)(2,1)S(1)} %fusion.108) | copy-start | bytes 1179652
  240.9 57.3 %copy-start.75 = (bf16[256,768]{0,1:T(8,128)(2,1)}, bf16[256,768]{0,1:T(8,128)(2,1)S(1)}, u32[]{:S(2)}) copy-start(bf16[256,768]{0,1:T(8,128)(2,1)S(1)} %fusion.157) | copy-start | bytes 1179652
  309.7 56.7 %copy-start.69 = (bf16[256,3072]{1,0:T(8,128)(2,1)}, bf16[256,3072]{1,0:T(8,128)(2,1)S(1)}, u32[]{:S(2)}) copy-start(bf16[256,3072]{1,0:T(8,128)(2,1)S(1)} %get-tuple-element.124) | copy-start | bytes 4718596
  520.1 158.4 %reduce-scatter.22.cloned.1.call-start = ((), (), s32[]{:S(2)}) async-start(), calls=%async_computation.19 | async-start | bytes 1769472
  547.7 155.0 %reduce-scatter.16.cloned.1.call-start = ((), (), s32[]{:S(2)}) async-start(), calls=%async_computation.16 | async-start | bytes 1769472 | tf_op jit(solution)/shard_map/reduce_scatter | solution.py:226
  549.3 216.1 %reduce-scatter.18.cloned.1.call-start = ((), (), s32[]{:S(2)}) async-start(), calls=%async_computation.17 | async-start | bytes 7077888 | tf_op jit(solution)/shard_map/reduce_scatter | solution.py:238
  554.6 273.9 %reduce-scatter.20.cloned.1.call-start = ((), (), s32[]{:S(2)}) async-start(), calls=%async_computation.18 | async-start | bytes 7077888 | tf_op jit(solution)/shard_map/reduce_scatter | solution.py:244
  560.2 292.7 %reduce-scatter.24.cloned.1.call-start = ((), (), s32[]{:S(2)}) async-start(), calls=%async_computation.20 | async-start | bytes 1769472
  657.2 220.3 %reduce-scatter.26.cloned.1.call-start = ((), (), s32[]{:S(2)}) async-start(), calls=%async_computation.21 | async-start | bytes 1769472
  658.7 178.1 %copy-start.64 = (bf16[768,768]{1,0:T(8,128)(2,1)S(1)}, bf16[768,768]{1,0:T(8,128)(2,1)}, u32[]{:S(2)}) copy-start(bf16[768,768]{1,0:T(8,128)(2,1)} %all-gather.20.cloned.1.call-done) | copy-start | bytes 3538948
  (91 other events, 597.9 us)
Sparse Core Ops, SparseCore 0:
  9.6 24.8 all-gather.19
  36.0 22.7 all-gather.23
  60.4 22.9 all-gather.17
  86.0 62.2 all-gather.21
  151.0 60.4 all-gather.25
  212.9 20.9 all-gather.27
  235.5 62.6 all-gather.29
  299.7 62.5 all-gather.31
  520.3 133.8 reduce-scatter.13
  656.8 21.6 reduce-scatter.21
  680.9 21.7 reduce-scatter.15
  705.4 59.9 reduce-scatter.17
  768.4 59.9 reduce-scatter.19
  831.1 21.8 reduce-scatter.23
  855.8 21.6 reduce-scatter.25
where the time goes:
time: 1200 us
  waiting for transfers between devices  513 us (43%)
  blocking collectives  340 us (28%)
  matrix products  214 us (18%)
  other arithmetic  72.8 us (6%)
  local copies, waits for them, and re-layouts  38.5 us (3%)
  between operations  16.7 us (1%)
    psum x1, blocking collectives, on_device(): totals = lax.psum(tuple(shards), 'ctx')  304 us
    dot_general x30, matrix products, inner_rows(): lax.dot_general(left, right, (((1,), (1,)), ((), ())), preferred_element_...  94 us
    reduce_scatter x1, waiting for transfers between devices, on_device(): lax.psum_scatter(key_terms.astype(jnp.bfloat16), 'ctx', scatter_dimension...  93.9 us
    reduce_scatter x1, waiting for transfers between devices, on_device(): lax.psum_scatter(grad_outer.astype(jnp.bfloat16), 'fsdp', scatter_dimensi...  63 us
    reduce_scatter x1, waiting for transfers between devices, on_device(): lax.psum_scatter(grad_inner.astype(jnp.bfloat16), 'fsdp', scatter_dimensi...  62.7 us
    convert_element_type x12, other arithmetic, on_device(): d_scores = (probs * (d_probs - delta[:, None])).astype(jnp.bfloat16)  56.2 us
    all_gather x1, waiting for transfers between devices, on_device(): lax.all_gather(key_low, 'ctx', axis=0, tiled=True)  54.9 us
    all_gather x1, waiting for transfers between devices, on_device(): lax.all_gather(inner_weight, 'fsdp', axis=0, tiled=True)  54.8 us
  transfers between devices with their start and end apart: 15, of which 13 were waited for; matrix products, arithmetic and copies ran while one was open for 12% of the time, Pallas kernels for 0%

commit v1 on v0

--- a/solution.py
+++ b/solution.py
@@ -7,6 +7,18 @@
 H = 12
 HD = 64
 eps = 1e-12
+
+
+def collect(shard, axis, dim):
+    ways, here, lap = (lax.axis_size(axis), lax.axis_index(axis), shard.shape[dim])
+    shape = [n * ways if d == dim else n for d, n in enumerate(shard.shape)]
+    full = lax.dynamic_update_slice_in_dim(
+        jnp.zeros(shape, shard.dtype), shard, here * lap, axis=dim
+    )
+    for far in range(1, ways):
+        shard = lax.ppermute(shard, axis, [(d, (d + 1) % ways) for d in range(ways)])
+        full = lax.dynamic_update_slice_in_dim(full, shard, (here - far) % ways * lap, axis=dim)
+    return full
 
 
 def layer_norm(r, gain, shift):
@@ -115,7 +127,7 @@
     places_own = first_row + jnp.arange(rows, dtype=jnp.int32)
     segs_own = segment_of(places_own, doc_lengths[0])
     keys_all, values_all = (
-        lax.all_gather(key_low, "ctx", axis=0, tiled=True),
+        collect(key_low, "ctx", 0),
         lax.all_gather(value_low, "ctx", axis=0, tiled=True),
     )
     places_all = jnp.arange(length_total, dtype=jnp.int32)

time: 1200 us -> 1160 us (0.967)
  waiting for transfers between devices: 513 us -> 440 us
  local copies, waits for them, and re-layouts: 38.5 us -> 62.6 us
  starting transfers between devices: 1.07 us -> 13.2 us
    ppermute x0 -> x15, waiting for transfers between devices: none -> 110 us  [collect(): lax.ppermute(shard, axis, [(d, (d + 1) % ways) for d in range(ways)])]
    all_gather x1 -> x0, waiting for transfers between devices: 54.9 us -> none  [on_device(): lax.all_gather(key_low, 'ctx', axis=0, tiled=True)]
    all_gather x1, waiting for transfers between devices: 54.8 us -> 0.02 us  [on_device(): lax.all_gather(inner_weight, 'fsdp', axis=0, tiled=True)]
    all_gather x1, waiting for transfers between devices: 52.7 us -> 0.02 us  [on_device(): lax.all_gather(outer_weight, 'fsdp', axis=0, tiled=True)]
    convert_element_type x12, other arithmetic: 56.2 us -> 34.7 us  [on_device(): d_scores = (probs * (d_probs - delta[:, None])).astype(jnp.bfloat16)]
    all_gather x1, waiting for transfers between devices: 16.8 us -> 0.01 us  [on_device(): lax.all_gather(value_low, 'ctx', axis=0, tiled=True)]
    dynamic_update_slice x0 -> x15, local copies, waits for them, and re-layouts: none -> 15.7 us  [collect(): lax.dynamic_update_slice_in_dim(full, shard, (here - far) % ways * lap, a...]
    ppermute x0 -> x15, starting transfers between devices: none -> 12.2 us  [collect(): lax.ppermute(shard, axis, [(d, (d + 1) % ways) for d in range(ways)])]
  transfers between devices with their start and end apart: 15 -> 29, of which waited for: 13 -> 21; matrix products, arithmetic and copies ran while one was open for 12% -> 17% of each run, Pallas kernels for 0% -> 0%
where the time goes in v1:
time: 1160 us; the launch traced here: 1150 us
  waiting for transfers between devices  440 us (38%)
  blocking collectives  342 us (29%)
  matrix products  211 us (18%)
  other arithmetic  67.3 us (6%)
  local copies, waits for them, and re-layouts  62.6 us (5%)
  between operations  16.7 us (1%)
  starting transfers between devices  13.2 us (1%)
    psum x1, blocking collectives, on_device(): totals = lax.psum(tuple(shards), 'ctx')  304 us
    ppermute x15, waiting for transfers between devices, collect(): lax.ppermute(shard, axis, [(d, (d + 1) % ways) for d in range(ways)])  110 us
    reduce_scatter x1, waiting for transfers between devices, on_device(): lax.psum_scatter(key_terms.astype(jnp.bfloat16), 'ctx', scatter_dimension...  92.2 us
    dot_general x30, matrix products, inner_rows(): lax.dot_general(left, right, (((1,), (1,)), ((), ())), preferred_element_...  83.3 us
    reduce_scatter x1, waiting for transfers between devices, on_device(): lax.psum_scatter(grad_inner.astype(jnp.bfloat16), 'fsdp', scatter_dimensi...  62.9 us
    reduce_scatter x1, waiting for transfers between devices, on_device(): lax.psum_scatter(grad_outer.astype(jnp.bfloat16), 'fsdp', scatter_dimensi...  62.9 us
    dot_general x30, matrix products, inner_cols(): lax.dot_general(left, right, (((0,), (0,)), ((), ())), preferred_element_...  55.5 us
    unnamed x17, waiting for transfers between devices  47.9 us
  transfers between devices with their start and end apart: 29, of which 21 were waited for; matrix products, arithmetic and copies ran while one was open for 17% of the time, Pallas kernels for 0%

profile of v1, /device:TPU:1, one launch (start us, length us, event | category | flops | bytes accessed | tf_op | source)
XLA Modules:
  0.0 1152.6 jit_solution(4829131503897284451)
XLA Ops:
  13.9 20.5 %all-gather.21.cloned.1.call-done = bf16[768,768]{1,0:T(8,128)(2,1)} async-done(((bf16[384,768]{1,0:T(8,128)(2,1)}), bf16[768,768]{1,0:T(8,128)(2,1)}) %all-gather.21.cloned.1.call-update) | async-done | bytes 1179664 | tf_op jit(solution)/shard_map/all_gather | solution.py:85
  38.4 20.4 %all-gather.19.cloned.1.call-done = bf16[768,768]{1,0:T(8,128)(2,1)} async-done(((bf16[384,768]{1,0:T(8,128)(2,1)}), bf16[768,768]{1,0:T(8,128)(2,1)}) %all-gather.19.cloned.1.call-update) | async-done | bytes 1179664 | tf_op jit(solution)/shard_map/all_gather | solution.py:84
  79.2 5.5 collective-permute-done.2
  86.4 8.2 collective-permute-done.3
  94.7 16.0 %collective-permute-done.4 = bf16[256,768]{1,0:T(8,128)(2,1)S(1)} collective-permute-done((bf16[256,768]{1,0:T(8,128)(2,1)S(1)}, bf16[256,768]{1,0:T(8,128)(2,1)S(1)}, u32[]{:S(2)}, u32[]{:S(2)}) %collective-permute-start.4) | collective-permute-done | bytes 393248 | tf_op jit(solution)/shard_map/ppermute | solution.py:19
  110.7 10.9 collective-permute-done.5
  121.6 18.0 %collective-permute-done.6 = bf16[256,768]{1,0:T(8,128)(2,1)S(1)} collective-permute-done((bf16[256,768]{1,0:T(8,128)(2,1)S(1)}, bf16[256,768]{1,0:T(8,128)(2,1)S(1)}, u32[]{:S(2)}, u32[]{:S(2)}) %collective-permute-start.6) | collective-permute-done | bytes 393248 | tf_op jit(solution)/shard_map/ppermute | solution.py:19
  139.7 14.3 %collective-permute-done.7 = bf16[256,768]{1,0:T(8,128)(2,1)S(1)} collective-permute-done((bf16[256,768]{1,0:T(8,128)(2,1)S(1)}, bf16[256,768]{1,0:T(8,128)(2,1)S(1)}, u32[]{:S(2)}, u32[]{:S(2)}) %collective-permute-start.7) | collective-permute-done | bytes 393248 | tf_op jit(solution)/shard_map/ppermute | solution.py:19
  154.1 5.3 all-gather.6
  205.7 11.0 collective-permute-done.11
  219.8 7.0 collective-permute-done.12
  285.7 4.8 fusion.36
  333.3 11.7 %multiply_convert_fusion.12 = (bf16[256,3072]{1,0:T(8,128)(2,1)S(1)}, f32[256,3072]{1,0:T(8,128)}, f32[256,3072]{1,0:T(8,128)}) fusion(f32[3072]{0:T(1024)S(1)} %bitcast.86, bf16[768,3072]{1,0:T(8,128)(2,1)} %all-gather.27.cloned.1.call-done, f32[256,768]{1,0:T(8,128)S(1)} %get-tuple-element.154, f32[768]{0:T(1024)S(1)} %reshape.268, ...), kind=kOutput, calls=%fused_computation.174 | convolution fusion | flops 1260847104 | bytes 13389824 | tf_op jit(solution)/shard_map/dot_general | solution.py:161
  417.5 4.9 multiply_convert_fusion.1
  507.4 5.6 convolution_convert_fusion.1
  518.2 92.2 %reduce-scatter.14.cloned.1.call-done = bf16[256,1536]{0,1:T(8,128)(2,1)} async-done(((bf16[4096,1536]{0,1:T(8,128)(2,1)}), bf16[256,1536]{0,1:T(8,128)(2,1)}) %reduce-scatter.14.cloned.1.call-update) | async-done | bytes 786448 | tf_op jit(solution)/shard_map/reduce_scatter | solution.py:205
  625.1 9.8 reduce-scatter.22.cloned.1.call-done
  636.3 22.6 %reduce-scatter.16.cloned.1.call-done = bf16[384,768]{1,0:T(8,128)(2,1)} async-done(((bf16[768,768]{1,0:T(8,128)(2,1)}), bf16[384,768]{1,0:T(8,128)(2,1)}) %reduce-scatter.16.cloned.1.call-update) | async-done | bytes 589840 | tf_op jit(solution)/shard_map/reduce_scatter | solution.py:238
  658.9 62.9 %reduce-scatter.18.cloned.1.call-done = bf16[384,3072]{1,0:T(8,128)(2,1)} async-done(((bf16[768,3072]{1,0:T(8,128)(2,1)}), bf16[384,3072]{1,0:T(8,128)(2,1)}) %reduce-scatter.18.cloned.1.call-update) | async-done | bytes 2359312 | tf_op jit(solution)/shard_map/reduce_scatter | solution.py:250
  721.8 62.9 %reduce-scatter.20.cloned.1.call-done = bf16[1536,768]{1,0:T(8,128)(2,1)} async-done(((bf16[3072,768]{1,0:T(8,128)(2,1)}), bf16[1536,768]{1,0:T(8,128)(2,1)}) %reduce-scatter.20.cloned.1.call-update) | async-done | bytes 2359312 | tf_op jit(solution)/shard_map/reduce_scatter | solution.py:256
  784.9 6.1 all-reduce.10
  797.6 11.6 %reduce-scatter.24.cloned.1.call-done = bf16[384,768]{1,0:T(8,128)(2,1)} async-done(((bf16[768,768]{1,0:T(8,128)(2,1)}), bf16[384,768]{1,0:T(8,128)(2,1)}) %reduce-scatter.24.cloned.1.call-update) | async-done | bytes 589840
  810.6 23.3 %reduce-scatter.26.cloned.1.call-done = bf16[384,768]{1,0:T(8,128)(2,1)} async-done(((bf16[768,768]{1,0:T(8,128)(2,1)}), bf16[384,768]{1,0:T(8,128)(2,1)}) %reduce-scatter.26.cloned.1.call-update) | async-done | bytes 589840
  835.2 303.9 %all-reduce.12 = (f32[384,768]{0,1:T(8,128)}, f32[384]{0:T(512)}, f32[384,768]{0,1:T(8,128)}, f32[384,768]{0,1:T(8,128)S(1)}, f32[384]{0:T(512)}, /*index=5*/f32...) all-reduce(bf16[384,768]{0,1:T(8,128)(2,1)S(1)} %copy.52, ...), channel_id=1, replica_groups=mesh['ctx'=16,'fsdp'=2] {'ctx'}, use_global_device_ids=true, to_apply=%region_49.50 | all-reduce | flops 3543552 | bytes 21270528 | tf_op jit(solution)/shard_map/psum | solution.py:269
  (478 shorter events, 376.3 us)
Async XLA Ops:
  7.2 27.3 %all-gather.21.cloned.1.call-start = ((), (), s32[]{:S(2)}) async-start(), calls=%async_computation.9 | async-start | bytes 1769472 | tf_op jit(solution)/shard_map/all_gather | solution.py:85
  7.9 50.9 %all-gather.19.cloned.1.call-start = ((), (), s32[]{:S(2)}) async-start(), calls=%async_computation.8 | async-start | bytes 1769472 | tf_op jit(solution)/shard_map/all_gather | solution.py:84
  8.7 193.6 %all-gather.17.cloned.1.call-start = ((), (), s32[]{:S(2)}) async-start(), calls=%async_computation.7 | async-start | bytes 1769472 | tf_op jit(solution)/shard_map/all_gather | solution.py:82
  9.4 292.5 %all-gather.23.cloned.1.call-start = ((), (), s32[]{:S(2)}) async-start(), calls=%async_computation.10 | async-start | bytes 6684672 | tf_op jit(solution)/shard_map/all_gather | solution.py:131
  37.1 293.9 %all-gather.25.cloned.1.call-start = ((), (), s32[]{:S(2)}) async-start(), calls=%async_computation.11 | async-start | bytes 1769472 | tf_op jit(solution)/shard_map/all_gather | solution.py:87
  37.7 295.5 %all-gather.27.cloned.1.call-start = ((), (), s32[]{:S(2)}) async-start(), calls=%async_computation.12 | async-start | bytes 7077888 | tf_op jit(solution)/shard_map/all_gather | solution.py:91
  38.3 306.7 %all-gather.29.cloned.1.call-start = ((), (), s32[]{:S(2)}) async-start(), calls=%async_computation.13 | async-start | bytes 7077888 | tf_op jit(solution)/shard_map/all_gather | solution.py:93
  94.7 16.0 %collective-permute-start.4 = (bf16[256,768]{1,0:T(8,128)(2,1)S(1)}, bf16[256,768]{1,0:T(8,128)(2,1)S(1)}, u32[]{:S(2)}, u32[]{:S(2)}) collective-permute-start(bf16[256,768]{1,0:T(8,128)(2,1)S(1)} %collective-permute-done.3), channel_id=1, source_target_pairs={{0,2},{2,4},{4,6},{6,8},{8,10},{10,12},{12,14},{14,16},{16,18},{18... | collective-permute-start | bytes 1179656 | tf_op jit(solution)/shard_map/ppermute | solution.py:19
  110.7 10.9 collective-permute-start.5
  121.6 18.1 %collective-permute-start.6 = (bf16[256,768]{1,0:T(8,128)(2,1)S(1)}, bf16[256,768]{1,0:T(8,128)(2,1)S(1)}, u32[]{:S(2)}, u32[]{:S(2)}) collective-permute-start(bf16[256,768]{1,0:T(8,128)(2,1)S(1)} %collective-permute-done.5), channel_id=1, source_target_pairs={{0,2},{2,4},{4,6},{6,8},{8,10},{10,12},{12,14},{14,16},{16,18},{18... | collective-permute-start | bytes 1179656 | tf_op jit(solution)/shard_map/ppermute | solution.py:19
  139.7 14.3 %collective-permute-start.7 = (bf16[256,768]{1,0:T(8,128)(2,1)S(1)}, bf16[256,768]{1,0:T(8,128)(2,1)S(1)}, u32[]{:S(2)}, u32[]{:S(2)}) collective-permute-start(bf16[256,768]{1,0:T(8,128)(2,1)S(1)} %collective-permute-done.6), channel_id=1, source_target_pairs={{0,2},{2,4},{4,6},{6,8},{8,10},{10,12},{12,14},{14,16},{16,18},{18... | collective-permute-start | bytes 1179656 | tf_op jit(solution)/shard_map/ppermute | solution.py:19
  154.0 11.8 %collective-permute-start.8 = (bf16[256,768]{1,0:T(8,128)(2,1)S(1)}, bf16[256,768]{1,0:T(8,128)(2,1)}, u32[]{:S(2)}, u32[]{:S(2)}) collective-permute-start(bf16[256,768]{1,0:T(8,128)(2,1)S(1)} %collective-permute-done.7), channel_id=1, source_target_pairs={{0,2},{2,4},{4,6},{6,8},{8,10},{10,12},{12,14},{14,16},{16,18},{18... | collective-permute-start | bytes 1179656 | tf_op jit(solution)/shard_map/ppermute | solution.py:19
  154.0 456.4 %reduce-scatter.14.cloned.1.call-start = ((), (), s32[]{:S(2)}) async-start(), calls=%async_computation.14 | async-start | bytes 13369344 | tf_op jit(solution)/shard_map/reduce_scatter | solution.py:205
  165.8 17.1 %collective-permute-start.9 = (bf16[256,768]{1,0:T(8,128)(2,1)}, bf16[256,768]{1,0:T(8,128)(2,1)}, u32[]{:S(2)}, u32[]{:S(2)}) collective-permute-start(bf16[256,768]{1,0:T(8,128)(2,1)} %collective-permute-done.8), channel_id=1, source_target_pairs={{0,2},{2,4},{4,6},{6,8},{8,10},{10,12},{12,14},{14,16},{16,18},{18... | collective-permute-start | bytes 1179656 | tf_op jit(solution)/shard_map/ppermute | solution.py:19
  182.8 18.3 %collective-permute-start.10 = (bf16[256,768]{1,0:T(8,128)(2,1)}, bf16[256,768]{1,0:T(8,128)(2,1)}, u32[]{:S(2)}, u32[]{:S(2)}) collective-permute-start(bf16[256,768]{1,0:T(8,128)(2,1)} %collective-permute-done.9), channel_id=1, source_target_pairs={{0,2},{2,4},{4,6},{6,8},{8,10},{10,12},{12,14},{14,16},{16,18},{18... | collective-permute-start | bytes 1179656 | tf_op jit(solution)/shard_map/ppermute | solution.py:19
  201.2 15.6 %collective-permute-start.11 = (bf16[256,768]{1,0:T(8,128)(2,1)}, bf16[256,768]{1,0:T(8,128)(2,1)}, u32[]{:S(2)}, u32[]{:S(2)}) collective-permute-start(bf16[256,768]{1,0:T(8,128)(2,1)} %collective-permute-done.10), channel_id=1, source_target_pairs={{0,2},{2,4},{4,6},{6,8},{8,10},{10,12},{12,14},{14,16},{16,18},{18... | collective-permute-start | bytes 1179656 | tf_op jit(solution)/shard_map/ppermute | solution.py:19
  216.8 10.1 collective-permute-start.12
  236.7 10.1 collective-permute-start.14
  470.6 164.4 %reduce-scatter.22.cloned.1.call-start = ((), (), s32[]{:S(2)}) async-start(), calls=%async_computation.18 | async-start | bytes 1769472
  505.8 153.1 %reduce-scatter.16.cloned.1.call-start = ((), (), s32[]{:S(2)}) async-start(), calls=%async_computation.15 | async-start | bytes 1769472 | tf_op jit(solution)/shard_map/reduce_scatter | solution.py:238
  507.4 214.4 %reduce-scatter.18.cloned.1.call-start = ((), (), s32[]{:S(2)}) async-start(), calls=%async_computation.16 | async-start | bytes 7077888 | tf_op jit(solution)/shard_map/reduce_scatter | solution.py:250
  513.1 271.6 %reduce-scatter.20.cloned.1.call-start = ((), (), s32[]{:S(2)}) async-start(), calls=%async_computation.17 | async-start | bytes 7077888 | tf_op jit(solution)/shard_map/reduce_scatter | solution.py:256
  518.2 291.1 %reduce-scatter.24.cloned.1.call-start = ((), (), s32[]{:S(2)}) async-start(), calls=%async_computation.19 | async-start | bytes 1769472
  613.4 220.4 %reduce-scatter.26.cloned.1.call-start = ((), (), s32[]{:S(2)}) async-start(), calls=%async_computation.20 | async-start | bytes 1769472
  (110 other events, 1837.6 us)
Sparse Core Ops, SparseCore 0:
  9.6 24.8 all-gather.20
  36.0 22.7 all-gather.18
  60.4 22.7 all-gather.16
  85.9 69.9 all-gather.22
  157.3 23.7 all-gather.24
  182.5 62.7 all-gather.26
  246.8 62.7 all-gather.28
  470.7 139.6 reduce-scatter.13
  613.2 21.6 reduce-scatter.21
  637.1 21.7 reduce-scatter.15
  661.8 59.9 reduce-scatter.17
  724.6 59.9 reduce-scatter.19
  787.5 21.6 reduce-scatter.23
  812.0 21.8 reduce-scatter.25
